TPU v7x, 512 devices: a whole 4x8x8 slice. The times are simulated.
512 devices in a mesh: rep: 16 (over z, x_hi), exp: 32 (over y, x_lo, core).
Axes of the slice: x: 4 (x_hi: 2, x_lo: 2; x = x_hi * 2 + x_lo), y: 8, z: 8, core: 2. Of those that a mesh axis runs over, the one named last changes fastest.
Arguments:
- activations: bfloat16 [65536, 4096], P(('rep', 'exp')), may hold values from -6 to 6
- grad_hidden: bfloat16 [65536, 1024], P(('rep', 'exp')), may hold values from -6 to 6
- pre_gate: bfloat16 [65536, 1024], P(('rep', 'exp')), may hold values from -12 to 12
- pre_up: bfloat16 [65536, 1024], P(('rep', 'exp')), may hold values from -6 to 6
- modality: int32 [65536], P(('rep', 'exp')), may hold values from 0 to 1, as said below
- expert_index: int32 [65536], P(('rep', 'exp')), may hold values from 0 to 1
- master: float32 [16384, 2048], P(('exp', 'rep')), may hold values from -0.09375 to 0.09375
- first_moment: float32 [16384, 2048], P(('exp', 'rep')), may hold values from -18 to 18
- second_moment: float32 [16384, 2048], P(('exp', 'rep')), may hold values from 200 to 2000
Outputs:
- input_grad: bfloat16 [65536, 4096], P(('rep', 'exp'))
- new_master: float32 [16384, 2048], P(('exp', 'rep'))
- new_first: float32 [16384, 2048], P(('exp', 'rep'))
- new_second: float32 [16384, 2048], P(('exp', 'rep'))
Inputs may be any that keep to these rules, and one draw needn't show every extreme that they name: Among the 128 tokens of one device no expert 2 * modality + expert_index is named more than 48 times; in every replica group of 4096 tokens one expert is named exactly 48 times on every device.
All inputs are finite; a program needn't handle non-finite values.
Results may differ from a plain program's by a relative error of at most 0.019.
Values may be sent and summed in bfloat16 or wider, within the bound.
No kernel may reach another device: no remote copies, remote signals or barrier semaphores. Data moves between devices by JAX's collectives and lax.ppermute only.
A program may use at most 128 MiB of HBM per device.

v0:
```python
import jax
import jax.numpy as jnp
from jax import lax
from jax.sharding import PartitionSpec as P

EXPERTS = 4
CAP = 48
beta_one = 0.9
beta_two = 0.999
learn_rate = 0.02
adam_eps = 1e-08
adam_count = 1000


def from_partner(block, axis, stride):
    count = lax.axis_size(axis)
    route = []
    for low in range(count):
        high = low | 1 << stride
        if high != low and high < count:
            route += [(low, high), (high, low)]
    return lax.ppermute(block, axis, route)


def hidden_grads(saved_rows):
    grad_val = saved_rows[:, 0].astype(jnp.float32)
    gate_val = saved_rows[:, 1].astype(jnp.float32)
    up_val = saved_rows[:, 2].astype(jnp.float32)
    sig = 1.0 / (1.0 + jnp.exp(-gate_val))
    grad_gate = (grad_val * up_val * sig * (1.0 + gate_val * (1.0 - sig))).astype(jnp.bfloat16)
    grad_up = (grad_val * gate_val * sig).astype(jnp.bfloat16)
    return jnp.stack([grad_gate, grad_up], axis=1)


def body(
    activations,
    grad_hidden,
    pre_gate,
    pre_up,
    modality,
    expert_index,
    master,
    first_moment,
    second_moment,
):
    tok_count = activations.shape[0]
    width = activations.shape[1]
    hidden = grad_hidden.shape[1]
    exp_size = lax.axis_size("exp")
    group = exp_size // EXPERTS
    piece_width = width // group
    piece_hidden = hidden // group
    capacity = CAP
    rows_total = exp_size * capacity
    expert = 2 * modality + expert_index
    onehot = (expert[:, None] == jnp.arange(EXPERTS, dtype=jnp.int32)[None, :]).astype(jnp.int32)
    before = jnp.cumsum(onehot, axis=0) - onehot
    slot_pos = jnp.sum(before * onehot, axis=1)
    same_expert = expert[None, None, :] == jnp.arange(EXPERTS, dtype=jnp.int32)[:, None, None]
    same_slot = slot_pos[None, None, :] == jnp.arange(capacity, dtype=jnp.int32)[None, :, None]
    routing = (same_expert & same_slot).astype(jnp.bfloat16)
    x_split = activations.reshape(tok_count, group, piece_width)
    x_send = jnp.einsum("ect,tgd->egcd", routing, x_split, preferred_element_type=jnp.float32)
    x_send = x_send.astype(jnp.bfloat16).reshape(EXPERTS * group, capacity, piece_width)
    saved = jnp.stack([grad_hidden, pre_gate, pre_up], axis=1)
    split_saved = saved.reshape(tok_count, 3, group, piece_hidden)
    parts = jnp.einsum("ect,tsgh->egcsh", routing, split_saved, preferred_element_type=jnp.float32)
    parts = parts.astype(jnp.bfloat16).reshape(EXPERTS * group, capacity, 3 * piece_hidden)
    x_recv, h_recv = (
        lax.all_to_all(x_send, "exp", split_axis=0, concat_axis=0, tiled=True),
        lax.all_to_all(parts, "exp", split_axis=0, concat_axis=0, tiled=True),
    )
    local = hidden_grads(h_recv.reshape(rows_total, 3, piece_hidden))
    blocks = local[None]
    position = lax.axis_index("exp")
    for level in range(group.bit_length() - 1):
        partner = from_partner(blocks, "exp", level)
        upper = position // 2**level % 2 == 1
        blocks = jnp.where(
            upper,
            jnp.concatenate([partner, blocks], axis=0),
            jnp.concatenate([blocks, partner], axis=0),
        )
    grads_flat = jnp.transpose(blocks, (1, 2, 0, 3)).reshape(rows_total, 2 * hidden)
    x_rows = x_recv.reshape(rows_total, piece_width)
    shard_bf = master.astype(jnp.bfloat16)
    dx_rows = lax.dot_general(
        grads_flat,
        lax.all_gather(shard_bf, "rep", axis=0, tiled=True),
        (((1,), (1,)), ((), ())),
        preferred_element_type=jnp.float32,
    )
    dx_send = dx_rows.astype(jnp.bfloat16).reshape(exp_size, capacity, piece_width)
    back = lax.all_to_all(dx_send, "exp", split_axis=0, concat_axis=0, tiled=True)
    back = back.reshape(EXPERTS, group, capacity, piece_width)
    input_grad = jnp.einsum("ect,egcd->tgd", routing, back, preferred_element_type=jnp.float32)
    input_grad = input_grad.reshape(tok_count, width).astype(jnp.bfloat16)
    weight_grad = lax.psum_scatter(
        lax.dot_general(
            x_rows, grads_flat, (((0,), (0,)), ((), ())), preferred_element_type=jnp.float32
        ).astype(jnp.bfloat16),
        "rep",
        scatter_dimension=0,
        tiled=True,
    ).astype(jnp.float32)
    new_first = beta_one * first_moment + (1.0 - beta_one) * weight_grad
    new_second = beta_two * second_moment + (1.0 - beta_two) * weight_grad * weight_grad
    corr_one = 1.0 - beta_one**adam_count
    corr_two = 1.0 - beta_two**adam_count
    update = new_first / corr_one / (jnp.sqrt(new_second / corr_two) + adam_eps)
    new_master = master - learn_rate * update
    return (input_grad, new_master, new_first, new_second)


def solution(mesh):
    in_specs = (
        P(("rep", "exp"), None),
        P(("rep", "exp"), None),
        P(("rep", "exp"), None),
        P(("rep", "exp"), None),
        P(("rep", "exp")),
        P(("rep", "exp")),
        P(("exp", "rep"), None),
        P(("exp", "rep"), None),
        P(("exp", "rep"), None),
    )
    out_specs = (
        P(("rep", "exp"), None),
        P(("exp", "rep"), None),
        P(("exp", "rep"), None),
        P(("exp", "rep"), None),
    )
    return jax.shard_map(body, mesh=mesh, in_specs=in_specs, out_specs=out_specs, check_vma=False)
```

profile of v0, /device:TPU:1, one launch (start us, length us, event | category | flops | bytes accessed | tf_op | source)
XLA Modules:
  0.0 593.7 jit_solution(8257956728713181121)
XLA Ops:
  7.2 0.7 multiply_add_fusion
  8.4 1.1 copy.25
  9.7 1.1 copy.26
  11.4 0.5 fusion.2
  11.8 1.0 copy.31
  12.9 1.1 reshape.88
  13.9 41.6 %all_to_all.15 = bf16[32,48,384]{2,1,0:T(8,128)(2,1)} all-to-all(bf16[32,48,384]{2,1,0:T(8,128)(2,1)S(1)} %reshape.88), channel_id=1, replica_groups=mesh['rep'=16,'exp'=32] {'exp'}, dimensions={0} | all-to-all | bytes 2359296 | tf_op jit(solution)/shard_map/all_to_all | solution.py:71
  55.5 3.3 reshape.89
  58.8 1.7 fusion.30
  60.5 0.4 fusion.6
  61.1 2.9 collective-permute-start
  64.0 1.9 collective-permute-done
  65.9 0.3 maximum_select_fusion.2
  66.2 3.1 collective-permute-start.1
  69.3 34.4 %collective-permute-done.1 = bf16[2,1536,2,128]{3,1,2,0:T(8,128)(2,1)} collective-permute-done((bf16[2,1536,2,128]{3,1,2,0:T(8,128)(2,1)S(1)}, bf16[2,1536,2,128]{3,1,2,0:T(8,128)(2,1)}, u32[]{:S(2)}, u32[]{:S(2)}) %collective-permute-start.1) | collective-permute-done | bytes 1572896 | tf_op jit(solution)/shard_map/ppermute | solution.py:22
  103.8 3.1 maximum_select_fusion.1
  106.8 2.8 collective-permute-start.2
  109.6 1.7 convolution_convert_fusion.2
  111.3 5.8 all-to-all-start.2
  117.2 68.5 %collective-permute-done.2 = bf16[4,1536,2,128]{3,1,2,0:T(8,128)(2,1)} collective-permute-done((bf16[4,1536,2,128]{3,1,2,0:T(8,128)(2,1)S(1)}, bf16[4,1536,2,128]{3,1,2,0:T(8,128)(2,1)}, u32[]{:S(2)}, u32[]{:S(2)}) %collective-permute-start.2) | collective-permute-done | bytes 3145760 | tf_op jit(solution)/shard_map/ppermute | solution.py:22
  185.7 6.6 %fusion = bf16[1536,2,8,128]{3,0,1,2:T(8,128)(2,1)} fusion(bf16[4,1536,2,128]{3,1,2,0:T(8,128)(2,1)S(1)} %maximum_select_fusion.1, bf16[4,1536,2,128]{3,1,2,0:T(8,128)(2,1)} %collective-permute-done.2, pred[]{:T(512)S(6)} %eq.71), kind=kLoop, calls=%fused_computation.1 | loop fusion | flops 9437184 | bytes 12582913 | tf_op jit(solution)/shard_map/transpose | solution.py:84
  192.3 8.6 %copy.35 = bf16[1536,2,8,128]{0,3,2,1:T(8,128)(2,1)} copy(bf16[1536,2,8,128]{3,0,1,2:T(8,128)(2,1)} %fusion) | data formatting | bytes 12582912 | tf_op jit(solution)/shard_map/transpose | solution.py:84
  200.9 11.8 %all-to-all-done.2 = bf16[32,48,512]{2,1,0:T(8,128)(2,1)} async-done(((bf16[32,48,512]{2,1,0:T(8,128)(2,1)}), bf16[32,48,512]{2,1,0:T(8,128)(2,1)}, u32[]{:S(2)}, u32[]{:S(2)}) %all-to-all-start.2) | async-done | bytes 1572896 | tf_op jit(solution)/shard_map/all_to_all | solution.py:70
  212.7 8.1 %convolution_convert_fusion = bf16[512,2048]{1,0:T(8,128)(2,1)} fusion(bf16[1536,512]{1,0:T(8,128)(2,1)} %bitcast.20, bf16[1536,2048]{0,1:T(8,128)(2,1)} %bitcast.54), kind=kOutput, calls=%fused_computation.5 | convolution fusion | flops 3222274048 | bytes 9961472 | tf_op jit(solution)/shard_map/dot_general | solution.py:99
  221.1 210.8 %reduce-scatter.2.cloned.1.call-done = bf16[32,2048]{1,0:T(8,128)(2,1)} async-done(((bf16[512,2048]{1,0:T(8,128)(2,1)}), bf16[32,2048]{1,0:T(8,128)(2,1)}) %reduce-scatter.2.cloned.1.call-update) | async-done | bytes 131088 | tf_op jit(solution)/shard_map/reduce_scatter | solution.py:98
  431.9 1.9 multiply_subtract_fusion
  433.9 92.5 %all-gather.2.cloned.1.call-done = bf16[512,2048]{1,0:T(8,128)(2,1)} async-done(((bf16[32,2048]{1,0:T(8,128)(2,1)}), bf16[512,2048]{1,0:T(8,128)(2,1)}) %all-gather.2.cloned.1.call-update) | async-done | bytes 2097168 | tf_op jit(solution)/shard_map/all_gather | solution.py:89
  526.3 6.9 %convolution_convert_fusion.1 = bf16[1536,512]{1,0:T(8,128)(2,1)S(1)} fusion(bf16[1536,2048]{0,1:T(8,128)(2,1)} %bitcast.55, bf16[512,2048]{1,0:T(8,128)(2,1)} %all-gather.2.cloned.1.call-done), kind=kOutput, calls=%fused_computation.6 | convolution fusion | flops 3222011904 | bytes 9961472 | tf_op jit(solution)/shard_map/dot_general | solution.py:87
  533.2 50.5 %all_to_all.16 = bf16[32,48,512]{2,1,0:T(8,128)(2,1)S(1)} all-to-all(bf16[32,48,512]{2,1,0:T(8,128)(2,1)S(1)} %bitcast.59), channel_id=1, replica_groups=mesh['rep'=16,'exp'=32] {'exp'}, dimensions={0} | all-to-all | bytes 3145728 | tf_op jit(solution)/shard_map/all_to_all | solution.py:94
  583.8 0.9 copy.55
  584.6 0.8 dot_general.22
  585.4 1.5 fusion.1
  (26 shorter events, 1.6 us)
Async XLA Ops:
  7.2 3.8 copy-start.5
  61.1 4.8 collective-permute-start
  66.1 3.2 copy-start
  66.2 37.6 %collective-permute-start.1 = (bf16[2,1536,2,128]{3,1,2,0:T(8,128)(2,1)S(1)}, bf16[2,1536,2,128]{3,1,2,0:T(8,128)(2,1)}, u32[]{:S(2)}, u32[]{:S(2)}) collective-permute-start(bf16[2,1536,2,128]{3,1,2,0:T(8,128)(2,1)S(1)} %maximum_select_fusion.2), channel_id=1, source_target_pairs={{0,2},{2,0},{1,3},{3,1},{4,6},{6,4},{5,7},{7,5},{8,10},{10,8},{9,1... | collective-permute-start | bytes 4718600 | tf_op jit(solution)/shard_map/ppermute | solution.py:22
  69.3 40.3 %copy-start.1 = (bf16[128,4096]{1,0:T(8,128)(2,1)S(1)}, bf16[128,4096]{1,0:T(8,128)(2,1)}, u32[]{:S(2)}) copy-start(bf16[128,4096]{1,0:T(8,128)(2,1)} %param.9) | copy-start | bytes 3145732
  106.8 78.8 %collective-permute-start.2 = (bf16[4,1536,2,128]{3,1,2,0:T(8,128)(2,1)S(1)}, bf16[4,1536,2,128]{3,1,2,0:T(8,128)(2,1)}, u32[]{:S(2)}, u32[]{:S(2)}) collective-permute-start(bf16[4,1536,2,128]{3,1,2,0:T(8,128)(2,1)S(1)} %maximum_select_fusion.1), channel_id=1, source_target_pairs={{0,4},{4,0},{1,5},{5,1},{2,6},{6,2},{3,7},{7,3},{8,12},{12,8},{9,1... | collective-permute-start | bytes 9437192 | tf_op jit(solution)/shard_map/ppermute | solution.py:22
  111.3 101.4 %all-to-all-start.2 = ((bf16[32,48,512]{2,1,0:T(8,128)(2,1)}), bf16[32,48,512]{2,1,0:T(8,128)(2,1)}, u32[]{:S(2)}, u32[]{:S(2)}) async-start(bf16[32,48,512]{2,1,0:T(8,128)(2,1)} %bitcast.56), calls=%async_computation.2 | async-start | bytes 3145728 | tf_op jit(solution)/shard_map/all_to_all | solution.py:70
  117.1 314.8 %reduce-scatter.2.cloned.1.call-start = ((), (), s32[]{:S(2)}) async-start(), calls=%async_computation.5 | async-start | bytes 2228224 | tf_op jit(solution)/shard_map/reduce_scatter | solution.py:98
  220.8 211.1 %copy-start.2 = (f32[32,2048]{1,0:T(8,128)S(1)}, f32[32,2048]{1,0:T(8,128)}, u32[]{:S(2)}) copy-start(f32[32,2048]{1,0:T(8,128)} %param.15) | copy-start | bytes 786436
  220.8 211.1 %copy-start.3 = (f32[32,2048]{1,0:T(8,128)S(1)}, f32[32,2048]{1,0:T(8,128)}, u32[]{:S(2)}) copy-start(f32[32,2048]{1,0:T(8,128)} %param.17) | copy-start | bytes 786436
  220.8 211.1 %copy-start.4 = (f32[32,2048]{1,0:T(8,128)S(1)}, f32[32,2048]{1,0:T(8,128)}, u32[]{:S(2)}) copy-start(f32[32,2048]{1,0:T(8,128)} %param.16) | copy-start | bytes 786436
  220.8 305.5 %all-gather.2.cloned.1.call-start = ((), (), s32[]{:S(2)}) async-start(), calls=%async_computation.4 | async-start | bytes 2228224 | tf_op jit(solution)/shard_map/all_gather | solution.py:89
Sparse Core Ops, SparseCore 0:
  221.0 210.9 reduce-scatter.1
  435.6 90.6 all-gather.1
where the time goes:
time: 595 us; the launch traced here: 594 us
  waiting for transfers between devices  420 us (71%)
  blocking collectives  92.1 us (15%)
  local copies, waits for them, and re-layouts  20.4 us (3%)
  matrix products  18.6 us (3%)
  starting transfers between devices  14.8 us (2%)
  between operations  14.3 us (2%)
  other arithmetic  13.6 us (2%)
    reduce_scatter x1, waiting for transfers between devices, body(): lax.psum_scatter(lax.dot_general(x_rows, grads_flat, (((0,), (0,)), ((),...  211 us
    ppermute x3, waiting for transfers between devices, from_partner(): return lax.ppermute(block, axis, route)  105 us
    all_gather x1, waiting for transfers between devices, body(): lax.all_gather(shard_bf, 'rep', axis=0, tiled=True)  92.5 us
    all_to_all x1, blocking collectives, body(): lax.all_to_all(dx_send, 'exp', split_axis=0, concat_axis=0, tiled=True)  50.5 us
    all_to_all x1, blocking collectives, body(): lax.all_to_all(parts, 'exp', split_axis=0, concat_axis=0, tiled=True)  41.6 us
  transfers between devices with their start and end apart: 6, of which 6 were waited for; matrix products, arithmetic and copies ran while one was open for 3% of the time, Pallas kernels for 0%

commit v1 on v0

--- a/solution.py
+++ b/solution.py
@@ -10,6 +10,13 @@
 learn_rate = 0.02
 adam_eps = 1e-08
 adam_count = 1000
+
+
+def prepare_sources_all(field_in):
+    steps_seen = []
+    for _ in range(lax.axis_size("rep")):
+        steps_seen.append(field_in)
+    return jnp.concatenate(lax.all_to_all(jnp.stack(steps_seen), "rep", 0, 0), axis=0)
 
 
 def from_partner(block, axis, stride):
@@ -86,7 +93,7 @@
     shard_bf = master.astype(jnp.bfloat16)
     dx_rows = lax.dot_general(
         grads_flat,
-        lax.all_gather(shard_bf, "rep", axis=0, tiled=True),
+        prepare_sources_all(shard_bf),
         (((1,), (1,)), ((), ())),
         preferred_element_type=jnp.float32,
     )

time: 595 us -> 554 us (0.931)
  waiting for transfers between devices: 420 us -> 327 us
  blocking collectives: 92.1 us -> 148 us
    all_gather x1 -> x0, waiting for transfers between devices: 92.5 us -> none  [body(): lax.all_gather(shard_bf, 'rep', axis=0, tiled=True)]
    all_to_all x0 -> x1, blocking collectives: none -> 51.1 us  [prepare_sources_all(): lax.all_to_all(jnp.stack(steps_seen), 'rep', 0, 0)]
  transfers between devices with their start and end apart: 6 -> 5, of which waited for: 6 -> 5; matrix products, arithmetic and copies ran while one was open for 3% -> 3% of each run, Pallas kernels for 0% -> 0%
where the time goes in v1:
time: 554 us
  waiting for transfers between devices  327 us (59%)
  blocking collectives  148 us (27%)
  local copies, waits for them, and re-layouts  20.6 us (4%)
  matrix products  15.2 us (3%)
  starting transfers between devices  14.8 us (3%)
  between operations  14.3 us (3%)
  other arithmetic  13.6 us (2%)
    reduce_scatter x1, waiting for transfers between devices, body(): lax.psum_scatter(lax.dot_general(x_rows, grads_flat, (((0,), (0,)), ((),...  211 us
    ppermute x3, waiting for transfers between devices, from_partner(): return lax.ppermute(block, axis, route)  105 us
    all_to_all x1, blocking collectives, body(): lax.all_to_all(dx_send, 'exp', split_axis=0, concat_axis=0, tiled=True)  54.9 us
    all_to_all x1, blocking collectives, prepare_sources_all(): lax.all_to_all(jnp.stack(steps_seen), 'rep', 0, 0)  51.1 us
    all_to_all x1, blocking collectives, body(): lax.all_to_all(parts, 'exp', split_axis=0, concat_axis=0, tiled=True)  41.6 us
    all_to_all x1, waiting for transfers between devices, body(): lax.all_to_all(x_send, 'exp', split_axis=0, concat_axis=0, tiled=True)  11.7 us
  transfers between devices with their start and end apart: 5, of which 5 were waited for; matrix products, arithmetic and copies ran while one was open for 3% of the time, Pallas kernels for 0%

profile of v1, /device:TPU:1, one launch (start us, length us, event | category | flops | bytes accessed | tf_op | source)
XLA Modules:
  0.0 553.5 jit_solution(2445574595005367190)
XLA Ops:
  7.2 0.7 multiply_add_fusion
  8.4 1.1 copy.25
  9.7 1.1 copy.26
  11.4 0.5 fusion.2
  11.8 1.0 copy.31
  12.9 1.1 reshape.93
  13.9 41.6 %all_to_all.20 = bf16[32,48,384]{2,1,0:T(8,128)(2,1)} all-to-all(bf16[32,48,384]{2,1,0:T(8,128)(2,1)S(1)} %reshape.93), channel_id=1, replica_groups=mesh['rep'=16,'exp'=32] {'exp'}, dimensions={0} | all-to-all | bytes 2359296 | tf_op jit(solution)/shard_map/all_to_all | solution.py:78
  55.5 3.3 reshape.94
  58.8 1.7 fusion.30
  60.5 0.4 fusion.6
  61.1 2.9 collective-permute-start
  64.0 1.9 collective-permute-done
  65.9 0.3 maximum_select_fusion.2
  66.2 3.1 collective-permute-start.1
  69.3 34.4 %collective-permute-done.1 = bf16[2,1536,2,128]{3,1,2,0:T(8,128)(2,1)} collective-permute-done((bf16[2,1536,2,128]{3,1,2,0:T(8,128)(2,1)S(1)}, bf16[2,1536,2,128]{3,1,2,0:T(8,128)(2,1)}, u32[]{:S(2)}, u32[]{:S(2)}) %collective-permute-start.1) | collective-permute-done | bytes 1572896 | tf_op jit(solution)/shard_map/ppermute | solution.py:29
  103.8 3.1 maximum_select_fusion.1
  106.9 2.8 collective-permute-start.2
  109.6 1.7 convolution_convert_fusion.2
  111.4 5.8 %all-to-all-start.3 = ((bf16[32,48,512]{2,1,0:T(8,128)(2,1)}), bf16[32,48,512]{2,1,0:T(8,128)(2,1)}, u32[]{:S(2)}, u32[]{:S(2)}) async-start(bf16[32,48,512]{2,1,0:T(8,128)(2,1)} %bitcast.57), calls=%async_computation.3 | async-start | bytes 3145728 | tf_op jit(solution)/shard_map/all_to_all | solution.py:77
  117.4 68.3 %collective-permute-done.2 = bf16[4,1536,2,128]{3,1,2,0:T(8,128)(2,1)} collective-permute-done((bf16[4,1536,2,128]{3,1,2,0:T(8,128)(2,1)S(1)}, bf16[4,1536,2,128]{3,1,2,0:T(8,128)(2,1)}, u32[]{:S(2)}, u32[]{:S(2)}) %collective-permute-start.2) | collective-permute-done | bytes 3145760 | tf_op jit(solution)/shard_map/ppermute | solution.py:29
  185.7 6.7 %fusion = bf16[1536,2,8,128]{3,0,1,2:T(8,128)(2,1)} fusion(bf16[4,1536,2,128]{3,1,2,0:T(8,128)(2,1)S(1)} %maximum_select_fusion.1, bf16[4,1536,2,128]{3,1,2,0:T(8,128)(2,1)} %collective-permute-done.2, pred[]{:T(512)S(6)} %eq.71), kind=kLoop, calls=%fused_computation.1 | loop fusion | flops 9437184 | bytes 12582913 | tf_op jit(solution)/shard_map/transpose | solution.py:91
  192.4 8.6 %copy.35 = bf16[1536,2,8,128]{0,3,2,1:T(8,128)(2,1)} copy(bf16[1536,2,8,128]{3,0,1,2:T(8,128)(2,1)} %fusion) | data formatting | bytes 12582912 | tf_op jit(solution)/shard_map/transpose | solution.py:91
  201.0 11.7 %all-to-all-done.3 = bf16[32,48,512]{2,1,0:T(8,128)(2,1)} async-done(((bf16[32,48,512]{2,1,0:T(8,128)(2,1)}), bf16[32,48,512]{2,1,0:T(8,128)(2,1)}, u32[]{:S(2)}, u32[]{:S(2)}) %all-to-all-start.3) | async-done | bytes 1572896 | tf_op jit(solution)/shard_map/all_to_all | solution.py:77
  212.7 8.1 %convolution_convert_fusion = bf16[512,2048]{1,0:T(8,128)(2,1)} fusion(bf16[1536,512]{1,0:T(8,128)(2,1)} %bitcast.21, bf16[1536,2048]{0,1:T(8,128)(2,1)} %bitcast.55), kind=kOutput, calls=%fused_computation.5 | convolution fusion | flops 3222274048 | bytes 9961472 | tf_op jit(solution)/shard_map/dot_general | solution.py:106
  220.9 211.0 %reduce-scatter.2.cloned.1.call-done = bf16[32,2048]{1,0:T(8,128)(2,1)} async-done(((bf16[512,2048]{1,0:T(8,128)(2,1)}), bf16[32,2048]{1,0:T(8,128)(2,1)}) %reduce-scatter.2.cloned.1.call-update) | async-done | bytes 131088 | tf_op jit(solution)/shard_map/reduce_scatter | solution.py:105
  431.9 1.9 multiply_subtract_fusion
  434.0 51.1 %all_to_all.21 = bf16[16,32,2048]{2,1,0:T(8,128)(2,1)S(1)} all-to-all(bf16[16,32,2048]{2,1,0:T(8,128)(2,1)S(1)} %stack.17), channel_id=1, replica_groups=mesh['rep'=16,'exp'=32] {'rep'}, dimensions={0} | all-to-all | bytes 4194304 | tf_op jit(solution)/shard_map/all_to_all | solution.py:19
  485.2 3.5 convolution_convert_fusion.1
  488.6 54.9 %all_to_all.22 = bf16[32,48,512]{2,1,0:T(8,128)(2,1)S(1)} all-to-all(bf16[32,48,512]{2,1,0:T(8,128)(2,1)S(1)} %bitcast.61), channel_id=1, replica_groups=mesh['rep'=16,'exp'=32] {'exp'}, dimensions={0} | all-to-all | bytes 3145728 | tf_op jit(solution)/shard_map/all_to_all | solution.py:101
  543.6 0.9 copy.55
  544.4 0.8 dot_general.22
  545.2 1.5 fusion.1
  (27 shorter events, 1.7 us)
Async XLA Ops:
  7.2 3.8 copy-start.6
  61.1 4.8 collective-permute-start
  66.2 3.2 copy-start.1
  66.2 37.6 %collective-permute-start.1 = (bf16[2,1536,2,128]{3,1,2,0:T(8,128)(2,1)S(1)}, bf16[2,1536,2,128]{3,1,2,0:T(8,128)(2,1)}, u32[]{:S(2)}, u32[]{:S(2)}) collective-permute-start(bf16[2,1536,2,128]{3,1,2,0:T(8,128)(2,1)S(1)} %maximum_select_fusion.2), channel_id=1, source_target_pairs={{0,2},{2,0},{1,3},{3,1},{4,6},{6,4},{5,7},{7,5},{8,10},{10,8},{9,1... | collective-permute-start | bytes 4718600 | tf_op jit(solution)/shard_map/ppermute | solution.py:29
  69.3 40.3 %copy-start.2 = (bf16[128,4096]{1,0:T(8,128)(2,1)S(1)}, bf16[128,4096]{1,0:T(8,128)(2,1)}, u32[]{:S(2)}) copy-start(bf16[128,4096]{1,0:T(8,128)(2,1)} %param.9) | copy-start | bytes 3145732
  106.9 78.8 %collective-permute-start.2 = (bf16[4,1536,2,128]{3,1,2,0:T(8,128)(2,1)S(1)}, bf16[4,1536,2,128]{3,1,2,0:T(8,128)(2,1)}, u32[]{:S(2)}, u32[]{:S(2)}) collective-permute-start(bf16[4,1536,2,128]{3,1,2,0:T(8,128)(2,1)S(1)} %maximum_select_fusion.1), channel_id=1, source_target_pairs={{0,4},{4,0},{1,5},{5,1},{2,6},{6,2},{3,7},{7,3},{8,12},{12,8},{9,1... | collective-permute-start | bytes 9437192 | tf_op jit(solution)/shard_map/ppermute | solution.py:29
  111.4 101.4 %all-to-all-start.3 = ((bf16[32,48,512]{2,1,0:T(8,128)(2,1)}), bf16[32,48,512]{2,1,0:T(8,128)(2,1)}, u32[]{:S(2)}, u32[]{:S(2)}) async-start(bf16[32,48,512]{2,1,0:T(8,128)(2,1)} %bitcast.57), calls=%async_computation.3 | async-start | bytes 3145728 | tf_op jit(solution)/shard_map/all_to_all | solution.py:77
  117.1 314.7 %reduce-scatter.2.cloned.1.call-start = ((), (), s32[]{:S(2)}) async-start(), calls=%async_computation.5 | async-start | bytes 2228224 | tf_op jit(solution)/shard_map/reduce_scatter | solution.py:105
  220.8 211.0 %copy-start.3 = (f32[32,2048]{1,0:T(8,128)S(1)}, f32[32,2048]{1,0:T(8,128)}, u32[]{:S(2)}) copy-start(f32[32,2048]{1,0:T(8,128)} %param.15) | copy-start | bytes 786436
  220.8 211.0 %copy-start.4 = (f32[32,2048]{1,0:T(8,128)S(1)}, f32[32,2048]{1,0:T(8,128)}, u32[]{:S(2)}) copy-start(f32[32,2048]{1,0:T(8,128)} %param.17) | copy-start | bytes 786436
  220.8 211.0 %copy-start.5 = (f32[32,2048]{1,0:T(8,128)S(1)}, f32[32,2048]{1,0:T(8,128)}, u32[]{:S(2)}) copy-start(f32[32,2048]{1,0:T(8,128)} %param.16) | copy-start | bytes 786436
  433.8 51.4 %copy-start = (bf16[1536,2,8,128]{0,3,2,1:T(8,128)(2,1)S(1)}, bf16[1536,2,8,128]{0,3,2,1:T(8,128)(2,1)}, u32[]{:S(2)}) copy-start(bf16[1536,2,8,128]{0,3,2,1:T(8,128)(2,1)} %copy.35) | copy-start | bytes 18874372
Sparse Core Ops, SparseCore 0:
  221.0 210.8 reduce-scatter.1
